TPU v7x, 32 devices: a whole 2x2x4 slice. The times are simulated.
32 devices in a mesh: grp: 2 (over y), chol: 4 (over z), orb: 4 (over x, core).
Axes of the slice: x: 2, y: 2, z: 4, core: 2. Of those that a mesh axis runs over, the one named last changes fastest.
Arguments:
- green: bfloat16 [32, 600, 896], P(('grp', 'chol'), None, 'orb'), parts along dimension 0, may hold values from -6 to 6
- half_chol: bfloat16 [80, 600, 896], P(('grp', 'chol'), None, 'orb'), parts along dimension 0, may hold values from -0.0078125 to 0.0078125
- chol_vec: bfloat16 [80, 896, 896], P(('grp', 'chol'), 'orb'), parts along dimension 0, may hold values from -0.0546875 to 0.0546875
- noise: float32 [32, 40], P('grp', 'chol'), parts along dimension 0, may hold values from -6 to 6
- order: int32 [32], P('grp'), parts along dimension 0, may hold values from 0 to 15, each once
- walkers: bfloat16 [32, 600, 896], P(('grp', 'chol'), None, 'orb'), parts along dimension 0, may hold values from -3 to 3
Outputs:
- force_bias: float32 [32, 40], P('grp', 'chol'), parts along dimension 0
- propagated: bfloat16 [32, 600, 896], P(('grp', 'chol'), None, 'orb'), parts along dimension 0
There are 2 independent parts, one for each index of `grp`. A program takes and returns all parts, laid end to end along the dimension named above; each array names one. Nothing has to cross between parts.
Inputs may be any that keep to these rules, and one draw needn't show every extreme that they name: order is a permutation of the 16 walkers.
All inputs are finite; a program needn't handle non-finite values.
Results may differ from a plain program's by a relative error of at most 0.0086.
Values may be sent and summed in bfloat16 or wider, within the bound.
No kernel may reach another device: no remote copies, remote signals or barrier semaphores. Data moves between devices by JAX's collectives and lax.ppermute only.
A program may use at most 64 MiB of HBM per device.

v0:
```python
import jax
import jax.numpy as jnp
from jax import lax
from jax.sharding import PartitionSpec as P

TERMS = 6


def body(green, half_chol, chol_vec, noise, order, walkers):
    walk_dev = walkers.shape[0]
    all_green = lax.all_gather(green, "chol", axis=0, tiled=True)
    chosen = jnp.take(all_green, order, axis=0)
    flat_green = chosen.reshape(chosen.shape[0], -1)
    flat_half = half_chol.reshape(half_chol.shape[0], -1)
    partial_value = lax.dot_general(
        flat_green, flat_half, (((1,), (1,)), ((), ())), preferred_element_type=jnp.float32
    )
    force_bias = lax.psum(partial_value, "orb")
    fields = (noise - force_bias).astype(jnp.bfloat16)
    flat_chol = chol_vec.reshape(chol_vec.shape[0], -1)
    summed = lax.psum_scatter(
        jnp.dot(fields, flat_chol, preferred_element_type=jnp.float32),
        "chol",
        scatter_dimension=0,
        tiled=True,
    )
    propagator = summed.astype(jnp.bfloat16).reshape(walk_dev, chol_vec.shape[1], chol_vec.shape[2])
    full_prop = lax.all_gather(propagator, "orb", axis=1, tiled=True)
    column_walkers = lax.all_to_all(walkers, "orb", split_axis=1, concat_axis=2, tiled=True)
    running = column_walkers.astype(jnp.float32)
    term_now = column_walkers
    for power in range(1, TERMS + 1):
        scaled = (
            jnp.einsum("wiq,wpq->wip", term_now, full_prop, preferred_element_type=jnp.float32)
            / power
        )
        running = running + scaled
        term_now = scaled.astype(jnp.bfloat16)
    propagated = lax.all_to_all(
        running.astype(jnp.bfloat16), "orb", split_axis=2, concat_axis=1, tiled=True
    )
    return (force_bias, propagated)


def solution(mesh):
    return jax.shard_map(
        body,
        mesh=mesh,
        in_specs=(
            P(("grp", "chol"), None, "orb"),
            P(("grp", "chol"), None, "orb"),
            P(("grp", "chol"), "orb", None),
            P("grp", "chol"),
            P("grp"),
            P(("grp", "chol"), None, "orb"),
        ),
        out_specs=(P("grp", "chol"), P(("grp", "chol"), None, "orb")),
        check_vma=False,
    )
```

profile of v0, /device:TPU:0, one launch (start us, length us, event | category | flops | bytes accessed | tf_op | source)
XLA Modules:
  0.0 681.0 jit_solution(1911006067594825877)
XLA Ops:
  8.0 2.7 pad.1
  10.7 5.1 copy.32
  17.0 82.5 %all-gather.3.cloned.1.call-done = bf16[16,600,224]{1,2,0:T(8,128)(2,1)} async-done(((bf16[4,600,224]{1,2,0:T(8,128)(2,1)}), bf16[16,600,224]{1,2,0:T(8,128)(2,1)}) %all-gather.3.cloned.1.call-update) | async-done | bytes 4300816 | tf_op jit(solution)/shard_map/all_gather | solution.py:11
  99.5 5.5 gather_fusion
  105.1 2.8 broadcast_select_fusion
  107.9 2.5 fusion.9
  110.4 6.9 %psum.7 = f32[16,10]{1,0:T(8,128)S(1)} all-reduce(f32[16,10]{1,0:T(8,128)S(1)} %fusion.9), channel_id=1, replica_groups=mesh['grp'=2,'chol'=4,'orb'=4] {'orb'}, use_global_device_ids=true, to_apply=%region_0.1 | all-reduce | flops 160 | bytes 1280 | tf_op jit(solution)/shard_map/psum | solution.py:18
  117.3 9.2 %fusion.22 = f32[16,200704]{1,0:T(8,128)} fusion(bf16[10,200704]{1,0:T(8,128)(2,1)} %bitcast.53, f32[16,10]{1,0:T(8,128)S(1)} %copy-done.5, f32[16,10]{1,0:T(8,128)S(1)} %psum.7), kind=kOutput, calls=%fused_computation.30 | convolution fusion | flops 64225600 | bytes 16860416 | tf_op jit(solution)/shard_map/dot_general | solution.py:22
  126.6 426.7 %all-reduce.2 = bf16[16,200704]{1,0:T(8,128)(2,1)} all-reduce(f32[16,200704]{1,0:T(8,128)} %fusion.22), channel_id=2, replica_groups=mesh['grp'=2,'chol'=4,'orb'=4] {'chol'}, use_global_device_ids=true, to_apply=%region_1.2.clone | all-reduce | flops 3211264 | bytes 19267584
  553.3 2.3 dynamic-slice_convert_fusion
  557.2 1.4 copy.20
  558.6 31.5 %all_to_all.36 = bf16[4,600,224]{2,0,1:T(4,128)(2,1)S(1)} all-to-all(bf16[4,600,224]{2,0,1:T(4,128)(2,1)S(1)} %copy.20), channel_id=1, replica_groups=mesh['grp'=2,'chol'=4,'orb'=4] {'orb'}, dimensions={1} | all-to-all | bytes 2150400 | tf_op jit(solution)/shard_map/all_to_all | solution.py:29
  590.7 2.2 all_to_all.29
  592.9 23.7 %all-gather.5.cloned.1.call-done = bf16[4,896,896]{2,1,0:T(8,128)(2,1)} async-done(((bf16[4,224,896]{2,1,0:T(8,128)(2,1)}), bf16[4,896,896]{2,1,0:T(8,128)(2,1)}) %all-gather.5.cloned.1.call-update) | async-done | bytes 6422544 | tf_op jit(solution)/shard_map/all_gather | solution.py:28
  616.6 5.5 fusion.31
  622.1 2.3 fusion.28
  624.3 2.3 fusion.14
  626.6 2.3 fusion.15
  628.9 3.6 fusion.16
  632.6 6.2 fusion.8
  638.8 3.0 copy.23
  641.8 25.3 %all_to_all.37 = bf16[4,150,896]{1,0,2:T(4,128)(2,1)S(1)} all-to-all(bf16[4,150,896]{1,0,2:T(4,128)(2,1)S(1)} %copy.23), channel_id=1, replica_groups=mesh['grp'=2,'chol'=4,'orb'=4] {'orb'}, dimensions={2} | all-to-all | bytes 2150400 | tf_op jit(solution)/shard_map/all_to_all | solution.py:39
  667.2 2.7 copy.30
  669.8 4.3 reshape.29
  (27 shorter events, 3.6 us)
Async XLA Ops:
  7.2 100.8 %copy-start = (bf16[10,600,224]{1,2,0:T(8,128)(2,1)S(1)}, bf16[10,600,224]{1,2,0:T(8,128)(2,1)}, u32[]{:S(2)}) copy-start(bf16[10,600,224]{1,2,0:T(8,128)(2,1)} %param.7) | copy-start | bytes 8064004
  7.2 92.4 %all-gather.3.cloned.1.call-start = ((), (), s32[]{:S(2)}) async-start(), calls=%async_computation.2 | async-start | bytes 5734400 | tf_op jit(solution)/shard_map/all_gather | solution.py:11
  7.9 608.6 %all-gather.5.cloned.1.call-start = ((), (), s32[]{:S(2)}) async-start(), calls=%async_computation.3 | async-start | bytes 8028160 | tf_op jit(solution)/shard_map/all_gather | solution.py:28
  10.7 5.1 copy-start.7
  10.7 6.3 copy-start.6
  107.9 9.4 %copy-start.5 = (f32[16,10]{1,0:T(8,128)S(1)}, f32[16,10]{1,0:T(8,128)}, u32[]{:S(2)}) copy-start(f32[16,10]{1,0:T(8,128)} %param.9) | copy-start | bytes 1924
  117.3 9.3 %copy-start.4 = (f32[16,10]{1,0:T(8,128)}, f32[16,10]{1,0:T(8,128)S(1)}, u32[]{:S(2)}) copy-start(f32[16,10]{1,0:T(8,128)S(1)} %psum.7) | copy-start | bytes 1924
  555.6 1.6 copy-start.3
  616.6 5.5 copy-start.2
  667.2 7.0 %copy-start.1 = (bf16[10,600,224]{1,2,0:T(8,128)(2,1)S(1)}, bf16[10,600,224]{1,2,0:T(8,128)(2,1)}, u32[]{:S(2)}) copy-start(bf16[10,600,224]{1,2,0:T(8,128)(2,1)} %param.7) | copy-start | bytes 8064004
Sparse Core Ops, SparseCore 0:
  9.6 89.9 all-gather.2
  557.1 59.3 all-gather.4
where the time goes:
time: 682 us; the launch traced here: 681 us
  blocking collectives  490 us (72%)
  waiting for transfers between devices  107 us (16%)
  matrix products  33.9 us (5%)
  local copies, waits for them, and re-layouts  32 us (5%)
  between operations  14.9 us (2%)
    unnamed x1, blocking collectives  427 us
    all_gather x1, waiting for transfers between devices, body(): all_green = lax.all_gather(green, 'chol', axis=0, tiled=True)  82.5 us
    all_to_all x1, blocking collectives, body(): lax.all_to_all(walkers, 'orb', split_axis=1, concat_axis=2, tiled=True)  31.5 us
    all_to_all x1, blocking collectives, body(): lax.all_to_all(running.astype(jnp.bfloat16), 'orb', split_axis=2, concat_...  25.3 us
    all_gather x1, waiting for transfers between devices, body(): full_prop = lax.all_gather(propagator, 'orb', axis=1, tiled=True)  23.7 us
    dot_general x6, matrix products, body(): jnp.einsum('wiq,wpq->wip', term_now, full_prop, preferred_element_type=jn...  22.2 us
    unnamed x23, local copies, waits for them, and re-layouts  18.3 us
  transfers between devices with their start and end apart: 2, of which 2 were waited for; matrix products, arithmetic and copies ran while one was open for 2% of the time, Pallas kernels for 0%

commit v1 on v0

v1 whole, which is shorter than its diff:
```python
import functools

import jax
import jax.numpy as jnp
from jax import lax
from jax.experimental import pallas as pl
from jax.experimental.pallas import tpu as pltpu
from jax.sharding import PartitionSpec as P

TERMS = 6
LANE = 128
TILE = 16
PLANES = 4
VMEM_BYTES = 56 * 1024 * 1024
f32 = jnp.float32
bf16 = jnp.bfloat16

END = [(0, 1), (1, 0), (2, 3), (3, 2)]
MID = [(1, 2), (2, 1)]
CORE_SWAP = [(0, 1), (1, 0), (2, 3), (3, 2)]
CHIP_SWAP = [(0, 2), (2, 0), (1, 3), (3, 1)]


def plain_body(green, half_chol, chol_vec, noise, order, walkers):
    walk_dev = walkers.shape[0]
    all_green = lax.all_gather(green, "chol", axis=0, tiled=True)
    stored = lax.dot_general(
        all_green, half_chol, (((1, 2), (1, 2)), ((), ())), preferred_element_type=f32
    )
    stored = lax.psum(stored, "orb")
    force_bias = jnp.take(stored, order, axis=0)
    fields = (noise - force_bias).astype(bf16)
    flat_chol = chol_vec.reshape(chol_vec.shape[0], -1)
    summed = lax.psum_scatter(
        jnp.dot(fields, flat_chol, preferred_element_type=f32),
        "chol",
        scatter_dimension=0,
        tiled=True,
    )
    propagator = summed.astype(bf16).reshape(walk_dev, chol_vec.shape[1], chol_vec.shape[2])
    full_prop = lax.all_gather(propagator, "orb", axis=1, tiled=True)
    column_walkers = lax.all_to_all(walkers, "orb", split_axis=1, concat_axis=2, tiled=True)
    running = column_walkers.astype(f32)
    term_now = column_walkers
    for power in range(1, TERMS + 1):
        scaled = jnp.einsum("wiq,wpq->wip", term_now, full_prop, preferred_element_type=f32) / power
        running = running + scaled
        term_now = scaled.astype(bf16)
    propagated = lax.all_to_all(
        running.astype(bf16), "orb", split_axis=2, concat_axis=1, tiled=True
    )
    return force_bias, propagated


def spec_vmem():
    return pl.BlockSpec(memory_space=pltpu.VMEM)


def spec_smem():
    return pl.BlockSpec(memory_space=pltpu.SMEM)


def pack(x):
    n, r, c = x.shape
    tiles = pl.cdiv(c, LANE)

    def kernel(x_ref, o_ref):
        for t in range(tiles):
            width = min(LANE, c - t * LANE)
            if width < LANE:
                o_ref[0, t] = jnp.zeros((r, LANE), x.dtype)
            o_ref[0, t, :, :width] = x_ref[0, :, t * LANE : t * LANE + width]

    return pl.pallas_call(
        kernel,
        out_shape=jax.ShapeDtypeStruct((n, tiles, r, LANE), x.dtype),
        grid=(n,),
        in_specs=[pl.BlockSpec((1, r, c), lambda i: (i, 0, 0))],
        out_specs=pl.BlockSpec((1, tiles, r, LANE), lambda i: (i, 0, 0, 0)),
        cost_estimate=pl.CostEstimate(flops=0, bytes_accessed=4 * x.size, transcendentals=0),
        name="pack",
    )(x)


def xor_order(x, orb):
    n, r, c = x.shape

    def kernel(orb_ref, x_ref, o_ref):
        o_ref[...] = x_ref[...]

    return pl.pallas_call(
        kernel,
        out_shape=jax.ShapeDtypeStruct(x.shape, x.dtype),
        grid_spec=pltpu.PrefetchScalarGridSpec(
            num_scalar_prefetch=1,
            grid=(n,),
            in_specs=[pl.BlockSpec((1, r, c), lambda i, o: (i ^ o[0], 0, 0))],
            out_specs=pl.BlockSpec((1, r, c), lambda i, o: (i, 0, 0)),
        ),
        cost_estimate=pl.CostEstimate(flops=0, bytes_accessed=4 * x.size, transcendentals=0),
        name="xor_order",
    )(orb, x)


def xor_exchange(blocks):
    across = lax.ppermute(blocks[2:4], "orb", CHIP_SWAP)
    beside = lax.ppermute(jnp.concatenate([blocks[1:2], across[1:2]]), "orb", CORE_SWAP)
    return blocks[0:1], beside[0:1], across[0:1], beside[1:2]


def prop_rows(place, fields, own, near, own_at, near_at, rows, far, recv):
    vecs, _, cols = own.shape
    packed = near.ndim == 4
    walk_all = fields.shape[0]
    walk_dev = walk_all // PLANES
    walk_out = 2 * walk_dev
    wide = vecs * TILE
    lane_tiles = cols // LANE

    def expand(place_ref, f_ref, x_scr):
        chol, orb = place_ref[0], place_ref[1]
        half = chol // 2
        row = lax.broadcasted_iota(jnp.int32, (walk_out * TILE, walk_all), 0) // TILE
        col = lax.broadcasted_iota(jnp.int32, (walk_out * TILE, walk_all), 1)
        side = (1 - half) if far else half
        plane = jnp.where(row < walk_dev, side * (PLANES - 1), side + 1)
        want = plane * walk_dev + ((row % walk_dev) ^ orb)
        pick = (want == col).astype(bf16)
        by_row = jnp.dot(pick, f_ref[...], preferred_element_type=f32).astype(bf16)
        vec = lax.broadcasted_iota(jnp.int32, (2 * vecs, 2 * wide), 0)
        col2 = lax.broadcasted_iota(jnp.int32, (2 * vecs, 2 * wide), 1) // TILE
        spread = (vec == col2).astype(bf16)
        full = jnp.dot(by_row, spread, preferred_element_type=f32)
        r = lax.broadcasted_iota(jnp.int32, (walk_out * TILE, 2 * wide), 0) % TILE
        c = lax.broadcasted_iota(jnp.int32, (walk_out * TILE, 2 * wide), 1) % TILE
        x_scr[...] = jnp.where(r == c, full, 0.0).astype(bf16)

    def kernel(place_ref, f_ref, own_ref, near_ref, *rest):
        if recv is None:
            o_ref, x_scr = rest
        else:
            recv_ref, o_ref, x_scr = rest

        @pl.when(pl.program_id(0) == 0)
        def _():
            expand(place_ref, f_ref, x_scr)

        x_own = x_scr[:, :wide]
        x_near = x_scr[:, wide:]
        for t in range(0, lane_tiles):
            at = slice(t * LANE, (t + 1) * LANE)
            mine = own_ref[:, :, at].reshape(wide, LANE)
            other = (near_ref[:, t] if packed else near_ref[:, :, at]).reshape(wide, LANE)
            total = jnp.dot(x_own, mine, preferred_element_type=f32)
            total = total + jnp.dot(x_near, other, preferred_element_type=f32)
            total = total.reshape(walk_out, TILE, LANE)
            if recv is not None:
                total = total + recv_ref[:, :, at].astype(f32)
            o_ref[:, :, at] = total.astype(bf16)

    if packed:
        near_spec = pl.BlockSpec(
            (vecs, lane_tiles, TILE, LANE), lambda i, p: (0, 0, near_at // TILE + i, 0)
        )
    else:
        near_spec = pl.BlockSpec((vecs, TILE, cols), lambda i, p: (0, near_at // TILE + i, 0))
    in_specs = [
        pl.BlockSpec(fields.shape, lambda i, p: (0, 0)),
        pl.BlockSpec((vecs, TILE, cols), lambda i, p: (0, own_at // TILE + i, 0)),
        near_spec,
    ]
    args = [fields, own, near]
    block = pl.BlockSpec((walk_out, TILE, cols), lambda i, p: (0, i, 0))
    if recv is not None:
        in_specs.append(block)
        args.append(recv)
    size = walk_out * rows * cols
    return pl.pallas_call(
        kernel,
        out_shape=jax.ShapeDtypeStruct((walk_out, rows, cols), bf16),
        grid_spec=pltpu.PrefetchScalarGridSpec(
            num_scalar_prefetch=1,
            grid=(rows // TILE,),
            in_specs=in_specs,
            out_specs=block,
            scratch_shapes=[pltpu.VMEM((walk_out * TILE, 2 * wide), bf16)],
        ),
        cost_estimate=pl.CostEstimate(
            flops=2 * size * 2 * vecs * TILE, bytes_accessed=2 * size, transcendentals=0
        ),
        name="prop_far" if far else "prop_near",
    )(place, *args)


def taylor(place, prop, starts, walk):
    q_all = prop[0][0].shape[2]
    block, occ = walk[0].shape[1:]
    flat = [piece for chunk in prop for piece in chunk]
    n_prop = len(flat)

    def kernel(place_ref, *refs):
        prop_refs = refs[:n_prop]
        walk_refs = refs[n_prop : n_prop + 4]
        o_ref, p_scr, t_a, t_b, run = refs[n_prop + 4 :]
        orb = place_ref[1]
        for d in range(4):
            at = pl.multiple_of((orb ^ d) * block, TILE)
            start = walk_refs[d][0]
            t_a[pl.ds(at, block), :] = start
            run[pl.ds(at, block), :] = start.astype(f32)
            for n, first in enumerate(starts):
                piece = prop_refs[4 * n + d]
                p_scr[pl.ds(pl.multiple_of(at + first, TILE), piece.shape[1]), :] = piece[0]
        for power in range(1, TERMS + 1):
            src, dst = (t_a, t_b) if power % 2 else (t_b, t_a)
            scale = 1.0 / power

            def rows(n, _, src=src, dst=dst, scale=scale):
                at = pl.ds(pl.multiple_of(n * block, TILE), block)
                term = jnp.dot(p_scr[at, :], src[...], preferred_element_type=f32) * scale
                run[at, :] += term
                dst[at, :] = term.astype(bf16)
                return 0

            lax.fori_loop(0, 4, rows, 0)
        for d in range(4):
            at = pl.multiple_of((orb ^ d) * block, TILE)
            o_ref[d] = run[pl.ds(at, block), :].astype(bf16)

    return pl.pallas_call(
        kernel,
        out_shape=jax.ShapeDtypeStruct((4, block, occ), bf16),
        in_specs=[spec_smem()] + [spec_vmem()] * (n_prop + 4),
        out_specs=spec_vmem(),
        scratch_shapes=[
            pltpu.VMEM((q_all, q_all), bf16),
            pltpu.VMEM((q_all, occ), bf16),
            pltpu.VMEM((q_all, occ), bf16),
            pltpu.VMEM((q_all, occ), f32),
        ],
        compiler_params=pltpu.CompilerParams(vmem_limit_bytes=VMEM_BYTES),
        cost_estimate=pl.CostEstimate(
            flops=2 * TERMS * q_all * q_all * occ, bytes_accessed=8 * q_all * occ, transcendentals=0
        ),
        name="taylor",
    )(place, *flat, *walk)


def line_body(green, half_chol, chol_vec, noise, order, walkers):
    chol = lax.axis_index("chol")
    orb = lax.axis_index("orb")
    outer = (chol == 0) | (chol == PLANES - 1)
    place = jnp.stack([chol, orb]).astype(jnp.int32)
    walk_dev = walkers.shape[0]
    vecs, rows, cols = chol_vec.shape
    walk_all = noise.shape[0]

    walk_t = xor_order(walkers.transpose(0, 2, 1), place[1:])
    walk_in = xor_exchange(walk_t)

    own_g = pack(green.transpose(0, 2, 1))
    packed_h = pack(half_chol.transpose(0, 2, 1))
    unit = own_g.size // (vecs * cols) // TILE * TILE
    chunk_rows = [unit, unit, unit, rows - 3 * unit]
    chunk_at = [0, unit, 2 * unit, 3 * unit]

    def chol_part(n):
        part = pack(chol_vec[:, chunk_at[n] : chunk_at[n] + chunk_rows[n], :])
        return part.reshape(own_g.shape)

    def as_part(x):
        return x.reshape(vecs, cols // LANE, unit, LANE)

    def contract(x):
        return lax.dot_general(
            x, packed_h, (((1, 2, 3), (1, 2, 3)), ((), ())), preferred_element_type=f32
        )

    end1 = lax.ppermute(own_g, "chol", END)
    mid1 = lax.ppermute(own_g, "chol", MID)
    noise_near = lax.ppermute(noise, "chol", END)
    part0, part1 = chol_part(0), chol_part(1)
    end1, mid1 = lax.optimization_barrier((end1, mid1))
    end2 = lax.ppermute(jnp.where(outer, part0, mid1), "chol", END)
    mid2 = lax.ppermute(end1, "chol", MID)
    dot_own, dot_1, dot_m1 = contract(own_g), contract(end1), contract(mid1)
    end2, mid2 = lax.optimization_barrier((end2, mid2))
    end3 = lax.ppermute(jnp.where(outer, part1, mid2), "chol", END)
    dot_e2, dot_m2 = contract(end2), contract(mid2)
    dot_e3 = contract(end3)
    stored = jnp.concatenate(
        [dot_own, dot_1, jnp.where(outer, dot_e2, dot_m1), jnp.where(outer, dot_e3, dot_m2)]
    )
    gap = (order // walk_dev) ^ chol
    slot = jnp.where((gap >= 2) & ~outer, 5 - gap, gap)
    at = slot * walk_dev + order % walk_dev
    hot = at[:, None] == jnp.arange(walk_all)[None, :]
    bias_part = jnp.sum(jnp.where(hot[:, :, None], stored[None], 0.0), axis=1)
    near_part = lax.ppermute(bias_part, "chol", END)
    both = jnp.concatenate([bias_part, near_part], axis=1)
    both = both + lax.ppermute(both, "orb", CORE_SWAP)
    both = both + lax.ppermute(both, "orb", CHIP_SWAP)
    force_bias = both[:, :vecs]
    fields = (jnp.concatenate([noise, noise_near], axis=1) - both).astype(bf16)

    rest_in, end3, _ = lax.optimization_barrier((chol_vec[:, 2 * unit :, :], end3, near_part))
    rest = lax.ppermute(rest_in, "chol", END)
    near = [as_part(end2), as_part(end3), rest, rest]
    near_at = [0, 0, 0, unit]

    prop_pieces = []
    came = []
    for n in range(4):
        args = (place, fields, chol_vec, near[n], chunk_at[n], near_at[n], chunk_rows[n])
        far = prop_rows(*args, True, None)
        if n >= 2:
            far, came[n - 2] = lax.optimization_barrier((far, came[n - 2]))
        came.append(lax.ppermute(far, "chol", MID))
    for n in range(4):
        args = (place, fields, chol_vec, near[n], chunk_at[n], near_at[n], chunk_rows[n])
        done = prop_rows(*args, False, came[n])
        handed = lax.ppermute(done[:walk_dev], "chol", END)
        mine = jnp.where(outer, handed, done[walk_dev:])
        prop_pieces.append(xor_exchange(mine))

    out_blocks = taylor(place, prop_pieces, chunk_at, walk_in)
    back = jnp.concatenate(xor_exchange(out_blocks))
    propagated = xor_order(back, place[1:]).transpose(0, 2, 1)
    return force_bias, propagated


def solution(mesh):
    def body(green, half_chol, chol_vec, noise, order, walkers):
        fits = (
            mesh.shape["chol"] == PLANES
            and mesh.shape["orb"] == 4
            and walkers.shape[0] == 4
            and chol_vec.shape[1] % TILE == 0
            and chol_vec.shape[2] % LANE == 0
        )
        if fits:
            tiles = pl.cdiv(green.shape[1], LANE) * LANE * green.shape[0] * green.shape[2]
            unit = tiles // (chol_vec.shape[0] * chol_vec.shape[2])
            fits = (
                unit * chol_vec.shape[0] * chol_vec.shape[2] == tiles
                and unit % TILE == 0
                and 0 < chol_vec.shape[1] - 3 * unit
            )
        chosen = line_body if fits else plain_body
        return chosen(green, half_chol, chol_vec, noise, order, walkers)

    return jax.shard_map(
        body,
        mesh=mesh,
        in_specs=(
            P(("grp", "chol"), None, "orb"),
            P(("grp", "chol"), None, "orb"),
            P(("grp", "chol"), "orb", None),
            P("grp", "chol"),
            P("grp"),
            P(("grp", "chol"), None, "orb"),
        ),
        out_specs=(P("grp", "chol"), P(("grp", "chol"), None, "orb")),
        check_vma=False,
    )
```

time: 682 us -> 286 us (0.42)
  blocking collectives: 490 us -> 0 us
  Pallas kernels: 0 us -> 85.9 us
  starting transfers between devices: 0.08 us -> 50.4 us
  matrix products: 33.9 us -> 17.3 us
  between operations: 14.9 us -> 0.95 us
  waiting for transfers between devices: 107 us -> 93.4 us
    unnamed x1 -> x0, blocking collectives: 427 us -> none
    all_gather x2 -> x0, waiting for transfers between devices: 106 us -> none  [the longest x1 82.5 us: body(): all_green = lax.all_gather(green, 'chol', axis=0, tiled=True)]
    ppermute x0 -> x30, waiting for transfers between devices: none -> 93.4 us  [the longest x1 26.5 us: line_body(): noise_near = lax.ppermute(noise, 'chol', END)]
    pallas_call x0 -> x15, Pallas kernels: none -> 85.9 us  [the longest x8 40.3 us: prop_rows(): pl.pallas_call(kernel, out_shape=jax.ShapeDtypeStruct((walk_out, rows, co...]
    all_to_all x2 -> x0, blocking collectives: 56.8 us -> none  [the longest x1 31.5 us: body(): lax.all_to_all(walkers, 'orb', split_axis=1, concat_axis=2, tiled=True)]
    ppermute x0 -> x30, starting transfers between devices: none -> 50.4 us  [the longest x4 18.3 us: line_body(): handed = lax.ppermute(done[:walk_dev], 'chol', END)]
    slice x0 -> x30, local copies, waits for them, and re-layouts: none -> 25.9 us  [the longest x13 8.35 us: xor_exchange(): return (blocks[0:1], beside[0:1], across[0:1], beside[1:2])]
    dot_general x8 -> x6, matrix products: 33.9 us -> 17.3 us  [contract(): lax.dot_general(x, packed_h, (((1, 2, 3), (1, 2, 3)), ((), ())), preferre...]
  transfers between devices with their start and end apart: 2 -> 30, of which waited for: 2 -> 11; matrix products, arithmetic and copies ran while one was open for 2% -> 15% of each run, Pallas kernels for 0% -> 22%
where the time goes in v1:
time: 286 us; the launch traced here: 284 us
  waiting for transfers between devices  93.4 us (33%)
  Pallas kernels  85.9 us (30%)
  starting transfers between devices  50.4 us (18%)
  local copies, waits for them, and re-layouts  29.1 us (10%)
  matrix products  17.3 us (6%)
  other arithmetic  7.01 us (2%)
    pallas_call x8, Pallas kernels, prop_rows(): pl.pallas_call(kernel, out_shape=jax.ShapeDtypeStruct((walk_out, rows, co...  40.3 us
    ppermute x1, waiting for transfers between devices, line_body(): noise_near = lax.ppermute(noise, 'chol', END)  26.5 us
    pallas_call x4, Pallas kernels, pack(): pl.pallas_call(kernel, out_shape=jax.ShapeDtypeStruct((n, tiles, r, LANE)...  23.2 us
    ppermute x6, waiting for transfers between devices, xor_exchange(): across = lax.ppermute(blocks[2:4], 'orb', CHIP_SWAP)  19.5 us
    ppermute x4, starting transfers between devices, line_body(): handed = lax.ppermute(done[:walk_dev], 'chol', END)  18.3 us
    dot_general x6, matrix products, contract(): lax.dot_general(x, packed_h, (((1, 2, 3), (1, 2, 3)), ((), ())), preferre...  17.3 us
    pallas_call x1, Pallas kernels, taylor(): pl.pallas_call(kernel, out_shape=jax.ShapeDtypeStruct((4, block, occ), bf...  15.6 us
    ppermute x1, waiting for transfers between devices, line_body(): end1 = lax.ppermute(own_g, 'chol', END)  15.3 us
  transfers between devices with their start and end apart: 30, of which 11 were waited for; matrix products, arithmetic and copies ran while one was open for 15% of the time, Pallas kernels for 22%

profile of v1, /device:TPU:0, one launch (start us, length us, event | category | flops | bytes accessed | tf_op | source)
XLA Modules:
  0.0 284.0 jit_solution(14400601668427960899)
XLA Ops:
  0.6 3.5 %pack.4 = bf16[4,5,224,128]{3,2,1,0:T(8,128)(2,1)} custom-call(bf16[4,224,600]{2,1,0:T(8,128)(2,1)} %bitcast.48), custom_call_target="tpu_custom_call" | custom-call | bytes 2150400 | tf_op jit(solution)/shard_map/pack/pallas_call | solution.py:74
  11.1 6.3 %pack.6 = bf16[10,7,64,128]{3,2,1,0:T(8,128)(2,1)} custom-call(bf16[10,64,896]{2,1,0:T(8,128)(2,1)} %get-tuple-element.25.x_ref), custom_call_target="tpu_custom_call" | custom-call | bytes 2293760 | tf_op jit(solution)/shard_map/pack/pallas_call | solution.py:74
  17.4 15.3 %collective-permute-done = bf16[4,5,224,128]{3,2,1,0:T(8,128)(2,1)} collective-permute-done((bf16[4,5,224,128]{3,2,1,0:T(8,128)(2,1)}, bf16[4,5,224,128]{3,2,1,0:T(8,128)(2,1)}, u32[]{:S(2)}, u32[]{:S(2)}) %collective-permute-start) | collective-permute-done | bytes 1146912 | tf_op jit(solution)/shard_map/ppermute | solution.py:279
  40.3 6.3 %pack.7 = bf16[10,7,64,128]{3,2,1,0:T(8,128)(2,1)} custom-call(bf16[10,64,896]{2,1,0:T(8,128)(2,1)} %get-tuple-element.24.x_ref), custom_call_target="tpu_custom_call" | custom-call | bytes 2293760 | tf_op jit(solution)/shard_map/pack/pallas_call | solution.py:74
  46.6 7.1 %pack.5 = bf16[10,5,224,128]{3,2,1,0:T(8,128)(2,1)} custom-call(bf16[10,224,600]{2,1,0:T(8,128)(2,1)} %bitcast.45), custom_call_target="tpu_custom_call" | custom-call | bytes 5376000 | tf_op jit(solution)/shard_map/pack/pallas_call | solution.py:74
  53.7 4.0 %fusion.18 = f32[4,10]{1,0:T(4,128)S(1)} fusion(bf16[10,5,224,128]{3,2,1,0:T(8,128)(2,1)} %pack.5, bf16[4,5,224,128]{3,2,1,0:T(8,128)(2,1)S(1)} %copy-done.10), kind=kOutput, calls=%fused_computation.21 | convolution fusion | flops 11468800 | bytes 4014240 | tf_op jit(solution)/shard_map/dot_general | solution.py:275
  63.3 5.0 %collective-permute-start.4 = (bf16[4,5,224,128]{3,2,1,0:T(8,128)(2,1)S(1)}, bf16[4,5,224,128]{3,2,1,0:T(8,128)(2,1)S(1)}, u32[]{:S(2)}, u32[]{:S(2)}) collective-permute-start(bf16[4,5,224,128]{3,2,1,0:T(8,128)(2,1)S(1)} %broadcast_select_fusion), channel_id=1, source_target_pairs={{0,4},{4,0},{8,12},{12,8},{1,5},{5,1},{9,13},{13,9},{2,6},{6,2},{1... | collective-permute-start | bytes 3440648 | tf_op jit(solution)/shard_map/ppermute | solution.py:288
  77.3 14.6 %collective-permute-done.4 = bf16[4,5,224,128]{3,2,1,0:T(8,128)(2,1)S(1)} collective-permute-done((bf16[4,5,224,128]{3,2,1,0:T(8,128)(2,1)S(1)}, bf16[4,5,224,128]{3,2,1,0:T(8,128)(2,1)S(1)}, u32[]{:S(2)}, u32[]{:S(2)}) %collective-permute-start.4) | collective-permute-done | bytes 1146912 | tf_op jit(solution)/shard_map/ppermute | solution.py:288
  101.2 3.4 %xor_order.2 = bf16[4,224,600]{2,1,0:T(8,128)(2,1)} custom-call(s32[1]{0:T(128)} %bitcast.16.orb_ref, bf16[4,224,600]{2,1,0:T(8,128)(2,1)} %bitcast.46), custom_call_target="tpu_custom_call" | custom-call | bytes 2150400 | tf_op jit(solution)/shard_map/xor_order/pallas_call | solution.py:91
  109.3 26.5 %collective-permute-done.8 = f32[16,10]{1,0:T(8,128)S(1)} collective-permute-done((f32[16,10]{1,0:T(8,128)S(1)}, f32[16,10]{1,0:T(8,128)S(1)}, u32[]{:S(2)}, u32[]{:S(2)}) %collective-permute-start.8) | collective-permute-done | bytes 672 | tf_op jit(solution)/shard_map/ppermute | solution.py:281
  136.5 5.6 %prop_far.7 = bf16[8,64,896]{2,1,0:T(8,128)(2,1)} custom-call(s32[2]{0:T(128)} %pad_add_fusion.place_ref, bf16[16,20]{1,0:T(8,128)(2,1)} %get-tuple-element.22.f_ref, bf16[10,224,896]{2,1,0:T(8,128)(2,1)} %own_ref.15, bf16[10,7,64,128]{3,2,1,0:T(8,128)(2,1)} %bitcast.41), custom_call_target="tpu_custom_call" | custom-call | flops 293601280 | bytes 917504 | tf_op jit(solution)/shard_map/prop_far/pallas_call | solution.py:178
  146.3 5.4 %prop_far.5 = bf16[8,64,896]{2,1,0:T(8,128)(2,1)} custom-call(s32[2]{0:T(128)} %pad_add_fusion.place_ref, bf16[16,20]{1,0:T(8,128)(2,1)} %get-tuple-element.22.f_ref, bf16[10,224,896]{2,1,0:T(8,128)(2,1)} %own_ref.15, bf16[10,7,64,128]{3,2,1,0:T(8,128)(2,1)} %bitcast.39), custom_call_target="tpu_custom_call" | custom-call | flops 293601280 | bytes 917504 | tf_op jit(solution)/shard_map/prop_far/pallas_call | solution.py:178
  154.7 3.6 %prop_far.6 = bf16[8,32,896]{2,1,0:T(8,128)(2,1)} custom-call(s32[2]{0:T(128)} %pad_add_fusion.place_ref, bf16[16,20]{1,0:T(8,128)(2,1)} %get-tuple-element.22.f_ref, bf16[10,224,896]{2,1,0:T(8,128)(2,1)} %own_ref.15, bf16[10,96,896]{2,1,0:T(8,128)(2,1)} %copy-done), custom_call_target="tpu_custom_call" | custom-call | flops 146800640 | bytes 458752 | tf_op jit(solution)/shard_map/prop_far/pallas_call | solution.py:178
  159.0 5.5 %prop_near.5 = bf16[8,64,896]{2,1,0:T(8,128)(2,1)} custom-call(s32[2]{0:T(128)} %pad_add_fusion.place_ref, bf16[16,20]{1,0:T(8,128)(2,1)} %get-tuple-element.22.f_ref, bf16[10,224,896]{2,1,0:T(8,128)(2,1)} %own_ref.15, bf16[10,7,64,128]{3,2,1,0:T(8,128)(2,1)} %bitcast.42, bf16[8,64,896]{2,1,0:T(8,128)(2,1)} %collective-permute-done.14.rest_0_), custom_call_target="tpu_custom_call" | custom-call | flops 293601280 | bytes 917504 | tf_op jit(solution)/shard_map/prop_near/pallas_call | solution.py:178
  166.4 11.9 %collective-permute-start.15 = (bf16[4,64,896]{2,1,0:T(8,128)(2,1)}, bf16[4,64,896]{2,1,0:T(8,128)(2,1)}, u32[]{:S(2)}, u32[]{:S(2)}) collective-permute-start(bf16[4,64,896]{2,1,0:T(8,128)(2,1)} %slice.226), channel_id=1, source_target_pairs={{0,4},{4,0},{8,12},{12,8},{1,5},{5,1},{9,13},{13,9},{2,6},{6,2},{1... | collective-permute-start | bytes 1376264 | tf_op jit(solution)/shard_map/ppermute | solution.py:322
  179.3 5.4 %prop_far.4 = bf16[8,64,896]{2,1,0:T(8,128)(2,1)} custom-call(s32[2]{0:T(128)} %pad_add_fusion.place_ref, bf16[16,20]{1,0:T(8,128)(2,1)} %get-tuple-element.22.f_ref, bf16[10,224,896]{2,1,0:T(8,128)(2,1)} %own_ref.15, bf16[10,96,896]{2,1,0:T(8,128)(2,1)} %copy-done), custom_call_target="tpu_custom_call" | custom-call | flops 293601280 | bytes 917504 | tf_op jit(solution)/shard_map/prop_far/pallas_call | solution.py:178
  185.4 5.5 %prop_near.4 = bf16[8,64,896]{2,1,0:T(8,128)(2,1)} custom-call(s32[2]{0:T(128)} %pad_add_fusion.place_ref, bf16[16,20]{1,0:T(8,128)(2,1)} %get-tuple-element.22.f_ref, bf16[10,224,896]{2,1,0:T(8,128)(2,1)} %own_ref.15, bf16[10,7,64,128]{3,2,1,0:T(8,128)(2,1)} %bitcast.40, bf16[8,64,896]{2,1,0:T(8,128)(2,1)} %collective-permute-done.10.rest_0_), custom_call_target="tpu_custom_call" | custom-call | flops 293601280 | bytes 917504 | tf_op jit(solution)/shard_map/prop_near/pallas_call | solution.py:178
  192.0 5.3 %collective-permute-start.11 = (bf16[4,64,896]{2,1,0:T(8,128)(2,1)S(1)}, bf16[4,64,896]{2,1,0:T(8,128)(2,1)S(1)}, u32[]{:S(2)}, u32[]{:S(2)}) collective-permute-start(bf16[4,64,896]{2,1,0:T(8,128)(2,1)S(1)} %slice.217), channel_id=1, source_target_pairs={{0,4},{4,0},{8,12},{12,8},{1,5},{5,1},{9,13},{13,9},{2,6},{6,2},{1... | collective-permute-start | bytes 1376264 | tf_op jit(solution)/shard_map/ppermute | solution.py:322
  198.0 3.7 %prop_near.7 = bf16[8,32,896]{2,1,0:T(8,128)(2,1)} custom-call(s32[2]{0:T(128)} %pad_add_fusion.place_ref, bf16[16,20]{1,0:T(8,128)(2,1)} %get-tuple-element.22.f_ref, bf16[10,224,896]{2,1,0:T(8,128)(2,1)} %own_ref.15, bf16[10,96,896]{2,1,0:T(8,128)(2,1)} %copy-done, bf16[8,32,896]{2,1,0:T(8,128)(2,1)} %copy-done.13), custom_call_target="tpu_custom_call" | custom-call | flops 146800640 | bytes 458752 | tf_op jit(solution)/shard_map/prop_near/pallas_call | solution.py:178
  216.2 5.5 %prop_near.6 = bf16[8,64,896]{2,1,0:T(8,128)(2,1)} custom-call(s32[2]{0:T(128)} %pad_add_fusion.place_ref, bf16[16,20]{1,0:T(8,128)(2,1)} %get-tuple-element.22.f_ref, bf16[10,224,896]{2,1,0:T(8,128)(2,1)} %own_ref.15, bf16[10,96,896]{2,1,0:T(8,128)(2,1)} %copy-done, bf16[8,64,896]{2,1,0:T(8,128)(2,1)} %copy-done.12), custom_call_target="tpu_custom_call" | custom-call | flops 293601280 | bytes 917504 | tf_op jit(solution)/shard_map/prop_near/pallas_call | solution.py:178
  225.1 10.3 %collective-permute-done.19 = bf16[4,64,896]{2,1,0:T(8,128)(2,1)S(1)} collective-permute-done((bf16[4,64,896]{2,1,0:T(8,128)(2,1)S(1)}, bf16[4,64,896]{2,1,0:T(8,128)(2,1)S(1)}, u32[]{:S(2)}, u32[]{:S(2)}) %collective-permute-start.19) | collective-permute-done | bytes 458784 | tf_op jit(solution)/shard_map/ppermute | solution.py:322
  237.7 4.5 %collective-permute-done.20 = bf16[2,64,896]{2,1,0:T(8,128)(2,1)S(1)} collective-permute-done((bf16[2,64,896]{2,1,0:T(8,128)(2,1)S(1)}, bf16[2,64,896]{2,1,0:T(8,128)(2,1)S(1)}, u32[]{:S(2)}, u32[]{:S(2)}) %collective-permute-start.20) | collective-permute-done | bytes 229408 | tf_op jit(solution)/shard_map/ppermute | solution.py:106
  245.2 15.6 %taylor.1 = bf16[4,224,600]{2,1,0:T(8,128)(2,1)} custom-call(s32[2]{0:T(128)} %pad_add_fusion.place_ref, bf16[1,64,896]{2,1,0:T(8,128)(2,1)} %get-tuple-element.43.refs_0_, bf16[1,64,896]{2,1,0:T(8,128)(2,1)} %get-tuple-element.55.refs_1_, bf16[1,64,896]{2,1,0:T(8,128)(2,1)} %get-tuple-element.56.refs_2_, bf16[1,64,896]{2,1,0:T(8,128)(2,1)} %get-tuple-element.54.refs_3_, ...), custom_call_target="tpu_custom_call" | custom-call | flops 5780275200 | bytes 4300800 | tf_op jit(solution)/shard_map/taylor/pallas_call | solution.py:230
  263.6 13.5 %collective-permute-done.28 = bf16[2,224,600]{2,1,0:T(8,128)(2,1)S(1)} collective-permute-done((bf16[2,224,600]{2,1,0:T(8,128)(2,1)S(1)}, bf16[2,224,600]{2,1,0:T(8,128)(2,1)S(1)}, u32[]{:S(2)}, u32[]{:S(2)}) %collective-permute-start.28) | collective-permute-done | bytes 537632 | tf_op jit(solution)/shard_map/ppermute | solution.py:106
  (142 shorter events, 89.6 us)
Async XLA Ops:
  4.1 28.6 %collective-permute-start = (bf16[4,5,224,128]{3,2,1,0:T(8,128)(2,1)}, bf16[4,5,224,128]{3,2,1,0:T(8,128)(2,1)}, u32[]{:S(2)}, u32[]{:S(2)}) collective-permute-start(bf16[4,5,224,128]{3,2,1,0:T(8,128)(2,1)} %pack.4), channel_id=1, source_target_pairs={{0,4},{4,0},{8,12},{12,8},{1,5},{5,1},{9,13},{13,9},{2,6},{6,2},{1... | collective-permute-start | bytes 3440648 | tf_op jit(solution)/shard_map/ppermute | solution.py:279
  7.2 25.6 %collective-permute-start.1 = (bf16[4,5,224,128]{3,2,1,0:T(8,128)(2,1)}, bf16[4,5,224,128]{3,2,1,0:T(8,128)(2,1)S(1)}, u32[]{:S(2)}, u32[]{:S(2)}) collective-permute-start(bf16[4,5,224,128]{3,2,1,0:T(8,128)(2,1)} %pack.4), channel_id=1, source_target_pairs={{4,8},{8,4},{5,9},{9,5},{6,10},{10,6},{7,11},{11,7},{20,24},{24,20... | collective-permute-start | bytes 3440648 | tf_op jit(solution)/shard_map/ppermute | solution.py:280
  35.2 28.0 %collective-permute-start.2 = (bf16[4,5,224,128]{3,2,1,0:T(8,128)(2,1)}, bf16[4,5,224,128]{3,2,1,0:T(8,128)(2,1)S(1)}, u32[]{:S(2)}, u32[]{:S(2)}) collective-permute-start(bf16[4,5,224,128]{3,2,1,0:T(8,128)(2,1)} %broadcast_select_fusion.1), channel_id=1, source_target_pairs={{0,4},{4,0},{8,12},{12,8},{1,5},{5,1},{9,13},{13,9},{2,6},{6,2},{1... | collective-permute-start | bytes 3440648 | tf_op jit(solution)/shard_map/ppermute | solution.py:284
  38.6 24.6 %collective-permute-start.3 = (bf16[4,5,224,128]{3,2,1,0:T(8,128)(2,1)}, bf16[4,5,224,128]{3,2,1,0:T(8,128)(2,1)}, u32[]{:S(2)}, u32[]{:S(2)}) collective-permute-start(bf16[4,5,224,128]{3,2,1,0:T(8,128)(2,1)} %collective-permute-done), channel_id=1, source_target_pairs={{4,8},{8,4},{5,9},{9,5},{6,10},{10,6},{7,11},{11,7},{20,24},{24,20... | collective-permute-start | bytes 3440648 | tf_op jit(solution)/shard_map/ppermute | solution.py:285
  63.3 28.6 %collective-permute-start.4 = (bf16[4,5,224,128]{3,2,1,0:T(8,128)(2,1)S(1)}, bf16[4,5,224,128]{3,2,1,0:T(8,128)(2,1)S(1)}, u32[]{:S(2)}, u32[]{:S(2)}) collective-permute-start(bf16[4,5,224,128]{3,2,1,0:T(8,128)(2,1)S(1)} %broadcast_select_fusion), channel_id=1, source_target_pairs={{0,4},{4,0},{8,12},{12,8},{1,5},{5,1},{9,13},{13,9},{2,6},{6,2},{1... | collective-permute-start | bytes 3440648 | tf_op jit(solution)/shard_map/ppermute | solution.py:288
  99.0 54.5 %collective-permute-start.9 = (bf16[10,96,896]{2,1,0:T(8,128)(2,1)}, bf16[10,96,896]{2,1,0:T(8,128)(2,1)S(1)}, u32[]{:S(2)}, u32[]{:S(2)}) collective-permute-start(bf16[10,96,896]{2,1,0:T(8,128)(2,1)} %slice.165), channel_id=1, source_target_pairs={{0,4},{4,0},{8,12},{12,8},{1,5},{5,1},{9,13},{13,9},{2,6},{6,2},{1... | collective-permute-start | bytes 5160968 | tf_op jit(solution)/shard_map/ppermute | solution.py:307
  100.0 8.1 %collective-permute-start.6 = (f32[16,20]{1,0:T(8,128)S(1)}, f32[16,20]{1,0:T(8,128)S(1)}, u32[]{:S(2)}, u32[]{:S(2)}) collective-permute-start(f32[16,20]{1,0:T(8,128)S(1)} %pad_maximum_fusion.8), channel_id=1, source_target_pairs={{0,1},{1,0},{2,3},{3,2},{4,5},{5,4},{6,7},{7,6},{8,9},{9,8},{10,11... | collective-permute-start | bytes 3848 | tf_op jit(solution)/shard_map/ppermute | solution.py:301
  100.0 35.8 %collective-permute-start.8 = (f32[16,10]{1,0:T(8,128)S(1)}, f32[16,10]{1,0:T(8,128)S(1)}, u32[]{:S(2)}, u32[]{:S(2)}) collective-permute-start(f32[16,10]{1,0:T(8,128)S(1)} %copy-done.14), channel_id=1, source_target_pairs={{0,4},{4,0},{8,12},{12,8},{1,5},{5,1},{9,13},{13,9},{2,6},{6,2},{1... | collective-permute-start | bytes 1928 | tf_op jit(solution)/shard_map/ppermute | solution.py:281
  106.6 37.9 %collective-permute-start.26 = (bf16[2,224,600]{2,1,0:T(8,128)(2,1)}, bf16[2,224,600]{2,1,0:T(8,128)(2,1)}, u32[]{:S(2)}, u32[]{:S(2)}) collective-permute-start(bf16[2,224,600]{2,1,0:T(8,128)(2,1)} %slice.255), channel_id=1, source_target_pairs={{0,2},{2,0},{1,3},{3,1},{4,6},{6,4},{5,7},{7,5},{8,10},{10,8},{9,1... | collective-permute-start | bytes 1612808 | tf_op jit(solution)/shard_map/ppermute | solution.py:106
  108.1 27.7 %collective-permute-start.7 = (f32[16,20]{1,0:T(8,128)S(1)}, f32[16,20]{1,0:T(8,128)S(1)}, u32[]{:S(2)}, u32[]{:S(2)}) collective-permute-start(f32[16,20]{1,0:T(8,128)S(1)} %fusion.79), channel_id=1, source_target_pairs={{0,2},{2,0},{1,3},{3,1},{4,6},{6,4},{5,7},{7,5},{8,10},{10,8},{9,1... | collective-permute-start | bytes 3848 | tf_op jit(solution)/shard_map/ppermute | solution.py:302
  142.1 16.3 %collective-permute-start.14 = (bf16[8,64,896]{2,1,0:T(8,128)(2,1)}, bf16[8,64,896]{2,1,0:T(8,128)(2,1)}, u32[]{:S(2)}, u32[]{:S(2)}) collective-permute-start(bf16[8,64,896]{2,1,0:T(8,128)(2,1)} %prop_far.7), channel_id=1, source_target_pairs={{4,8},{8,4},{5,9},{9,5},{6,10},{10,6},{7,11},{11,7},{20,24},{24,20... | collective-permute-start | bytes 2752520 | tf_op jit(solution)/shard_map/ppermute | solution.py:318
  151.7 32.9 %collective-permute-start.10 = (bf16[8,64,896]{2,1,0:T(8,128)(2,1)}, bf16[8,64,896]{2,1,0:T(8,128)(2,1)}, u32[]{:S(2)}, u32[]{:S(2)}) collective-permute-start(bf16[8,64,896]{2,1,0:T(8,128)(2,1)} %prop_far.5), channel_id=1, source_target_pairs={{4,8},{8,4},{5,9},{9,5},{6,10},{10,6},{7,11},{11,7},{20,24},{24,20... | collective-permute-start | bytes 2752520 | tf_op jit(solution)/shard_map/ppermute | solution.py:318
  153.4 25.0 %collective-permute-start.27 = (bf16[2,224,600]{2,1,0:T(8,128)(2,1)S(1)}, bf16[2,224,600]{2,1,0:T(8,128)(2,1)S(1)}, u32[]{:S(2)}, u32[]{:S(2)}) collective-permute-start(bf16[2,224,600]{2,1,0:T(8,128)(2,1)S(1)} %pad_maximum_fusion.1), channel_id=1, source_target_pairs={{0,1},{1,0},{2,3},{3,2},{4,5},{5,4},{6,7},{7,6},{8,9},{9,8},{10,11... | collective-permute-start | bytes 1612808 | tf_op jit(solution)/shard_map/ppermute | solution.py:107
  158.3 38.9 %collective-permute-start.22 = (bf16[8,32,896]{2,1,0:T(8,128)(2,1)}, bf16[8,32,896]{2,1,0:T(8,128)(2,1)S(1)}, u32[]{:S(2)}, u32[]{:S(2)}) collective-permute-start(bf16[8,32,896]{2,1,0:T(8,128)(2,1)} %prop_far.6), channel_id=1, source_target_pairs={{4,8},{8,4},{5,9},{9,5},{6,10},{10,6},{7,11},{11,7},{20,24},{24,20... | collective-permute-start | bytes 1376264 | tf_op jit(solution)/shard_map/ppermute | solution.py:318
  166.4 36.7 %collective-permute-start.15 = (bf16[4,64,896]{2,1,0:T(8,128)(2,1)}, bf16[4,64,896]{2,1,0:T(8,128)(2,1)}, u32[]{:S(2)}, u32[]{:S(2)}) collective-permute-start(bf16[4,64,896]{2,1,0:T(8,128)(2,1)} %slice.226), channel_id=1, source_target_pairs={{0,4},{4,0},{8,12},{12,8},{1,5},{5,1},{9,13},{13,9},{2,6},{6,2},{1... | collective-permute-start | bytes 1376264 | tf_op jit(solution)/shard_map/ppermute | solution.py:322
  184.6 30.7 %collective-permute-start.18 = (bf16[8,64,896]{2,1,0:T(8,128)(2,1)}, bf16[8,64,896]{2,1,0:T(8,128)(2,1)S(1)}, u32[]{:S(2)}, u32[]{:S(2)}) collective-permute-start(bf16[8,64,896]{2,1,0:T(8,128)(2,1)} %prop_far.4), channel_id=1, source_target_pairs={{4,8},{8,4},{5,9},{9,5},{6,10},{10,6},{7,11},{11,7},{20,24},{24,20... | collective-permute-start | bytes 2752520 | tf_op jit(solution)/shard_map/ppermute | solution.py:318
  192.0 14.4 %collective-permute-start.11 = (bf16[4,64,896]{2,1,0:T(8,128)(2,1)S(1)}, bf16[4,64,896]{2,1,0:T(8,128)(2,1)S(1)}, u32[]{:S(2)}, u32[]{:S(2)}) collective-permute-start(bf16[4,64,896]{2,1,0:T(8,128)(2,1)S(1)} %slice.217), channel_id=1, source_target_pairs={{0,4},{4,0},{8,12},{12,8},{1,5},{5,1},{9,13},{13,9},{2,6},{6,2},{1... | collective-permute-start | bytes 1376264 | tf_op jit(solution)/shard_map/ppermute | solution.py:322
  204.2 6.3 %collective-permute-start.16 = (bf16[2,64,896]{2,1,0:T(8,128)(2,1)S(1)}, bf16[2,64,896]{2,1,0:T(8,128)(2,1)S(1)}, u32[]{:S(2)}, u32[]{:S(2)}) collective-permute-start(bf16[2,64,896]{2,1,0:T(8,128)(2,1)S(1)} %slice.230), channel_id=1, source_target_pairs={{0,2},{2,0},{1,3},{3,1},{4,6},{6,4},{5,7},{7,5},{8,10},{10,8},{9,1... | collective-permute-start | bytes 688136 | tf_op jit(solution)/shard_map/ppermute | solution.py:106
  211.1 13.2 %collective-permute-start.17 = (bf16[2,64,896]{2,1,0:T(8,128)(2,1)S(1)}, bf16[2,64,896]{2,1,0:T(8,128)(2,1)S(1)}, u32[]{:S(2)}, u32[]{:S(2)}) collective-permute-start(bf16[2,64,896]{2,1,0:T(8,128)(2,1)S(1)} %pad_maximum_fusion.4), channel_id=1, source_target_pairs={{0,1},{1,0},{2,3},{3,2},{4,5},{5,4},{6,7},{7,6},{8,9},{9,8},{10,11... | collective-permute-start | bytes 688136 | tf_op jit(solution)/shard_map/ppermute | solution.py:107
  214.6 9.1 %collective-permute-start.25 = (bf16[2,32,896]{2,1,0:T(8,128)(2,1)S(1)}, bf16[2,32,896]{2,1,0:T(8,128)(2,1)S(1)}, u32[]{:S(2)}, u32[]{:S(2)}) collective-permute-start(bf16[2,32,896]{2,1,0:T(8,128)(2,1)S(1)} %pad_maximum_fusion.6), channel_id=1, source_target_pairs={{0,1},{1,0},{2,3},{3,2},{4,5},{5,4},{6,7},{7,6},{8,9},{9,8},{10,11... | collective-permute-start | bytes 344072 | tf_op jit(solution)/shard_map/ppermute | solution.py:107
  214.8 28.3 %collective-permute-start.13 = (bf16[2,64,896]{2,1,0:T(8,128)(2,1)S(1)}, bf16[2,64,896]{2,1,0:T(8,128)(2,1)S(1)}, u32[]{:S(2)}, u32[]{:S(2)}) collective-permute-start(bf16[2,64,896]{2,1,0:T(8,128)(2,1)S(1)} %pad_maximum_fusion.3), channel_id=1, source_target_pairs={{0,1},{1,0},{2,3},{3,2},{4,5},{5,4},{6,7},{7,6},{8,9},{9,8},{10,11... | collective-permute-start | bytes 688136 | tf_op jit(solution)/shard_map/ppermute | solution.py:107
  222.9 12.5 %collective-permute-start.19 = (bf16[4,64,896]{2,1,0:T(8,128)(2,1)S(1)}, bf16[4,64,896]{2,1,0:T(8,128)(2,1)S(1)}, u32[]{:S(2)}, u32[]{:S(2)}) collective-permute-start(bf16[4,64,896]{2,1,0:T(8,128)(2,1)S(1)} %slice.235), channel_id=1, source_target_pairs={{0,4},{4,0},{8,12},{12,8},{1,5},{5,1},{9,13},{13,9},{2,6},{6,2},{1... | collective-permute-start | bytes 1376264 | tf_op jit(solution)/shard_map/ppermute | solution.py:322
  235.5 6.7 %collective-permute-start.20 = (bf16[2,64,896]{2,1,0:T(8,128)(2,1)S(1)}, bf16[2,64,896]{2,1,0:T(8,128)(2,1)S(1)}, u32[]{:S(2)}, u32[]{:S(2)}) collective-permute-start(bf16[2,64,896]{2,1,0:T(8,128)(2,1)S(1)} %slice.239), channel_id=1, source_target_pairs={{0,2},{2,0},{1,3},{3,1},{4,6},{6,4},{5,7},{7,5},{8,10},{10,8},{9,1... | collective-permute-start | bytes 688136 | tf_op jit(solution)/shard_map/ppermute | solution.py:106
  262.0 15.1 %collective-permute-start.28 = (bf16[2,224,600]{2,1,0:T(8,128)(2,1)S(1)}, bf16[2,224,600]{2,1,0:T(8,128)(2,1)S(1)}, u32[]{:S(2)}, u32[]{:S(2)}) collective-permute-start(bf16[2,224,600]{2,1,0:T(8,128)(2,1)S(1)} %slice.262), channel_id=1, source_target_pairs={{0,2},{2,0},{1,3},{3,1},{4,6},{6,4},{5,7},{7,5},{8,10},{10,8},{9,1... | collective-permute-start | bytes 1612808 | tf_op jit(solution)/shard_map/ppermute | solution.py:106
  (22 other events, 113.3 us)
